TPU v7x, 512 devices: a whole 4x8x8 slice. The times are simulated.
512 devices in a mesh: col: 16 (over z, x_lo), row: 32 (over y, x_hi, core).
Axes of the slice: x: 4 (x_hi: 2, x_lo: 2; x = x_hi * 2 + x_lo), y: 8, z: 8, core: 2. Of those that a mesh axis runs over, the one named last changes fastest.
Arguments:
- inputs: bfloat16 [1024, 8192], P('row', 'col'), may hold values from -6 to 6
- grad_out: bfloat16 [1024, 8192], P('row', 'col'), may hold values from -6 to 6
- gate_pre: bfloat16 [1024, 16384], P('col', 'row'), may hold values from -8 to 8
- up_pre: bfloat16 [1024, 16384], P('col', 'row'), may hold values from -6 to 6
- gate_weight: bfloat16 [8192, 16384], P('col', 'row'), may hold values from -0.0625 to 0.0625
- up_weight: bfloat16 [8192, 16384], P('col', 'row'), may hold values from -0.0625 to 0.0625
- down_weight: bfloat16 [16384, 8192], P('row', 'col'), may hold values from -0.046875 to 0.046875
Outputs:
- input_grad: bfloat16 [1024, 8192], P('row', 'col')
- gate_grad: bfloat16 [8192, 16384], P('col', 'row')
- up_grad: bfloat16 [8192, 16384], P('col', 'row')
- down_grad: bfloat16 [16384, 8192], P('row', 'col')
All inputs are finite; a program needn't handle non-finite values.
Results may differ from a plain program's by a relative error of at most 0.0049.
Values may be sent and summed in bfloat16 or wider, within the bound.
A program may use at most 64 MiB of HBM per device.

v0:
```python
import math
import jax
import jax.numpy as jnp
from jax import lax
from jax.sharding import PartitionSpec as P


def swiglu_back(hidden_grad, gate_pre, up_pre):
    gate_val = gate_pre.astype(jnp.float32)
    up_val = up_pre.astype(jnp.float32)
    sigmoid_val = jax.nn.sigmoid(gate_val)
    silu_val = gate_val * sigmoid_val
    hidden = (silu_val * up_val).astype(jnp.bfloat16)
    up_term = (hidden_grad * silu_val).astype(jnp.bfloat16)
    gate_term = (
        hidden_grad * up_val * sigmoid_val * (1.0 + gate_val * (1.0 - sigmoid_val))
    ).astype(jnp.bfloat16)
    return (hidden, gate_term, up_term)


def per_device(inputs, grad_out, gate_pre, up_pre, gate_weight, up_weight, down_weight):
    total_tokens = grad_out.shape[0] * lax.axis_size("row")
    grad_scale = 1.0 / math.sqrt(total_tokens)
    grad_all, input_all = (
        lax.all_gather(grad_out, "row", axis=0, tiled=True),
        lax.all_gather(inputs, "row", axis=0, tiled=True),
    )
    partial_hidden = jnp.einsum(
        "td,fd->tf", grad_all, down_weight, preferred_element_type=jnp.float32
    )
    hidden_grad = lax.psum_scatter(partial_hidden, "col", scatter_dimension=0, tiled=True)
    hidden, gate_term, up_term = swiglu_back(hidden_grad, gate_pre, up_pre)
    hidden_all, gate_all, up_all = (
        lax.all_gather(hidden, "col", axis=0, tiled=True),
        lax.all_gather(gate_term, "col", axis=0, tiled=True),
        lax.all_gather(up_term, "col", axis=0, tiled=True),
    )
    down_grad = (
        jnp.einsum("tf,td->fd", hidden_all, grad_all, preferred_element_type=jnp.float32)
        * grad_scale
    ).astype(jnp.bfloat16)
    gate_sum = jnp.einsum("td,tf->df", input_all, gate_all, preferred_element_type=jnp.float32)
    up_sum = jnp.einsum("td,tf->df", input_all, up_all, preferred_element_type=jnp.float32)
    gate_grad = (gate_sum * grad_scale).astype(jnp.bfloat16)
    up_grad = (up_sum * grad_scale).astype(jnp.bfloat16)
    input_grad = lax.psum_scatter(
        jnp.einsum("tf,df->td", gate_all, gate_weight, preferred_element_type=jnp.float32)
        + jnp.einsum("tf,df->td", up_all, up_weight, preferred_element_type=jnp.float32),
        "row",
        scatter_dimension=0,
        tiled=True,
    ).astype(jnp.bfloat16)
    return (input_grad, gate_grad, up_grad, down_grad)


def solution(mesh):
    return jax.shard_map(
        per_device,
        mesh=mesh,
        in_specs=(
            P("row", "col"),
            P("row", "col"),
            P("col", "row"),
            P("col", "row"),
            P("col", "row"),
            P("col", "row"),
            P("row", "col"),
        ),
        out_specs=(P("row", "col"), P("col", "row"), P("col", "row"), P("row", "col")),
        check_vma=False,
    )
```

profile of v0, /device:TPU:16, one launch (start us, length us, event | category | flops | bytes accessed | tf_op | source)
XLA Modules:
  0.0 622.8 jit_solution(12379006136893260064)
XLA Ops:
  7.2 0.7 all-gather.6.cloned.1.call-update
  8.0 90.3 %all-gather.6.cloned.1.call-done = bf16[1024,512]{1,0:T(8,128)(2,1)} async-done(((bf16[32,512]{1,0:T(8,128)(2,1)}), bf16[1024,512]{1,0:T(8,128)(2,1)}) %all-gather.6.cloned.1.call-update) | async-done | bytes 1048592 | tf_op jit(solution)/shard_map/all_gather | solution.py:25
  98.3 3.3 fusion.13
  101.6 0.0 all-gather.8.cloned.1.call-start
  101.7 76.2 %reduce-scatter.3.cloned.1.call-done = f32[64,512]{1,0:T(8,128)} async-done(((f32[1024,512]{1,0:T(8,128)}), f32[64,512]{1,0:T(8,128)}) %reduce-scatter.3.cloned.1.call-update) | async-done | bytes 131088 | tf_op jit(solution)/shard_map/reduce_scatter | solution.py:31
  177.9 1.7 multiply_convert_fusion
  179.6 0.0 all-gather.10.cloned.1.call-start
  179.6 0.5 all-gather.10.cloned.1.call-update
  180.2 0.5 all-gather.12.cloned.1.call-update
  180.8 0.5 all-gather.14.cloned.1.call-update
  181.3 0.0 reduce-scatter.5.cloned.1.call-start
  181.4 69.2 %all-gather.8.cloned.1.call-done = bf16[1024,512]{1,0:T(8,128)(2,1)} async-done(((bf16[64,512]{1,0:T(8,128)(2,1)}), bf16[1024,512]{1,0:T(8,128)(2,1)}) %all-gather.8.cloned.1.call-update) | async-done | bytes 1048592 | tf_op jit(solution)/shard_map/all_gather | solution.py:35
  250.6 2.0 fusion.14
  252.5 72.6 %all-gather.10.cloned.1.call-done = bf16[1024,512]{1,0:T(8,128)(2,1)} async-done(((bf16[64,512]{1,0:T(8,128)(2,1)}), bf16[1024,512]{1,0:T(8,128)(2,1)}) %all-gather.10.cloned.1.call-update) | async-done | bytes 1048592 | tf_op jit(solution)/shard_map/all_gather | solution.py:36
  325.2 3.4 convolution_add_fusion
  328.7 82.4 %all-gather.12.cloned.1.call-done = bf16[1024,512]{1,0:T(8,128)(2,1)} async-done(((bf16[32,512]{1,0:T(8,128)(2,1)}), bf16[1024,512]{1,0:T(8,128)(2,1)}) %all-gather.12.cloned.1.call-update) | async-done | bytes 1048592 | tf_op jit(solution)/shard_map/all_gather | solution.py:26
  411.0 2.0 fusion.4
  413.0 1.0 copy.11
  414.0 2.0 fusion.3
  416.1 1.0 copy.12
  417.1 65.4 %all-gather.14.cloned.1.call-done = bf16[1024,512]{1,0:T(8,128)(2,1)} async-done(((bf16[64,512]{1,0:T(8,128)(2,1)}), bf16[1024,512]{1,0:T(8,128)(2,1)}) %all-gather.14.cloned.1.call-update) | async-done | bytes 1048592 | tf_op jit(solution)/shard_map/all_gather | solution.py:34
  482.4 2.8 fusion.2
  485.2 129.3 %reduce-scatter.5.cloned.1.call-done = f32[32,512]{1,0:T(8,128)} async-done(((f32[1024,512]{1,0:T(8,128)}), f32[32,512]{1,0:T(8,128)}) %reduce-scatter.5.cloned.1.call-update) | async-done | bytes 65552 | tf_op jit(solution)/shard_map/reduce_scatter | solution.py:46
  614.5 1.5 convert_element_type.37
  (21 shorter events, 0.2 us)
Async XLA Ops:
  7.2 91.1 %copy-start = (bf16[512,512]{1,0:T(8,128)(2,1)S(1)}, bf16[512,512]{1,0:T(8,128)(2,1)}, u32[]{:S(2)}) copy-start(bf16[512,512]{1,0:T(8,128)(2,1)} %param.13) | copy-start | bytes 1572868
  7.2 91.1 %all-gather.6.cloned.1.call-start = ((), (), s32[]{:S(2)}) async-start(), calls=%async_computation.2 | async-start | bytes 1081344 | tf_op jit(solution)/shard_map/all_gather | solution.py:25
  7.9 170.0 %copy-start.5 = (bf16[64,512]{1,0:T(8,128)(2,1)S(1)}, bf16[64,512]{1,0:T(8,128)(2,1)}, u32[]{:S(2)}) copy-start(bf16[64,512]{1,0:T(8,128)(2,1)} %param.9) | copy-start | bytes 196612
  7.9 170.0 %copy-start.6 = (bf16[64,512]{1,0:T(8,128)(2,1)S(1)}, bf16[64,512]{1,0:T(8,128)(2,1)}, u32[]{:S(2)}) copy-start(bf16[64,512]{1,0:T(8,128)(2,1)} %param.10) | copy-start | bytes 196612
  7.9 170.0 %reduce-scatter.3.cloned.1.call-start = ((), (), s32[]{:S(2)}) async-start(), calls=%async_computation.3 | async-start | bytes 2228224 | tf_op jit(solution)/shard_map/reduce_scatter | solution.py:31
  101.6 149.0 %copy-start.4 = (bf16[512,512]{1,0:T(8,128)(2,1)S(1)}, bf16[512,512]{1,0:T(8,128)(2,1)}, u32[]{:S(2)}) copy-start(bf16[512,512]{1,0:T(8,128)(2,1)} %param.11) | copy-start | bytes 1572868
  101.6 149.0 %all-gather.8.cloned.1.call-start = ((), (), s32[]{:S(2)}) async-start(), calls=%async_computation.4 | async-start | bytes 1114112 | tf_op jit(solution)/shard_map/all_gather | solution.py:35
  179.6 145.6 %all-gather.10.cloned.1.call-start = ((), (), s32[]{:S(2)}) async-start(), calls=%async_computation.5 | async-start | bytes 1114112 | tf_op jit(solution)/shard_map/all_gather | solution.py:36
  180.2 230.9 %all-gather.12.cloned.1.call-start = ((), (), s32[]{:S(2)}) async-start(), calls=%async_computation.7 | async-start | bytes 1081344 | tf_op jit(solution)/shard_map/all_gather | solution.py:26
  180.8 301.7 %all-gather.14.cloned.1.call-start = ((), (), s32[]{:S(2)}) async-start(), calls=%async_computation.8 | async-start | bytes 1114112 | tf_op jit(solution)/shard_map/all_gather | solution.py:34
  181.3 433.2 %reduce-scatter.5.cloned.1.call-start = ((), (), s32[]{:S(2)}) async-start(), calls=%async_computation.6 | async-start | bytes 2162688 | tf_op jit(solution)/shard_map/reduce_scatter | solution.py:46
  328.6 82.4 %copy-start.2 = (bf16[1024,512]{1,0:T(8,128)(2,1)S(1)}, bf16[1024,512]{1,0:T(8,128)(2,1)}, u32[]{:S(2)}) copy-start(bf16[1024,512]{1,0:T(8,128)(2,1)} %all-gather.8.cloned.1.call-done) | copy-start | bytes 3145732
  328.6 85.4 %copy-start.3 = (bf16[1024,512]{1,0:T(8,128)(2,1)S(1)}, bf16[1024,512]{1,0:T(8,128)(2,1)}, u32[]{:S(2)}) copy-start(bf16[1024,512]{1,0:T(8,128)(2,1)} %all-gather.10.cloned.1.call-done) | copy-start | bytes 3145732
  414.0 68.4 %copy-start.1 = (bf16[1024,512]{1,0:T(8,128)(2,1)S(1)}, bf16[1024,512]{1,0:T(8,128)(2,1)}, u32[]{:S(2)}) copy-start(bf16[1024,512]{1,0:T(8,128)(2,1)} %all-gather.6.cloned.1.call-done) | copy-start | bytes 3145732
Sparse Core Ops, SparseCore 0:
  11.4 86.8 all-gather.5
  101.7 76.1 reduce-scatter.2
  180.6 69.9 all-gather.7
  253.1 72.0 all-gather.9
  328.4 82.5 all-gather.11
  413.0 69.4 all-gather.13
  487.2 127.3 reduce-scatter.4
where the time goes:
time: 623 us
  waiting for transfers between devices  588 us (94%)
  matrix products  15.4 us (2%)
  between operations  14.2 us (2%)
    reduce_scatter x1, waiting for transfers between devices, per_device(): lax.psum_scatter(jnp.einsum('tf,df->td', gate_all, gate_weight, preferred...  129 us
    all_gather x1, waiting for transfers between devices, per_device(): lax.all_gather(grad_out, 'row', axis=0, tiled=True)  90.3 us
    all_gather x1, waiting for transfers between devices, per_device(): lax.all_gather(inputs, 'row', axis=0, tiled=True)  82.4 us
    reduce_scatter x1, waiting for transfers between devices, per_device(): lax.psum_scatter(partial_hidden, 'col', scatter_dimension=0, tiled=True)  76.2 us
    all_gather x1, waiting for transfers between devices, per_device(): lax.all_gather(up_term, 'col', axis=0, tiled=True)  72.6 us
    all_gather x1, waiting for transfers between devices, per_device(): lax.all_gather(gate_term, 'col', axis=0, tiled=True)  69.2 us
    all_gather x1, waiting for transfers between devices, per_device(): lax.all_gather(hidden, 'col', axis=0, tiled=True)  65.4 us
  transfers between devices with their start and end apart: 7, of which 7 were waited for; matrix products, arithmetic and copies ran while one was open for 2% of the time, Pallas kernels for 0%

commit v1 on v0

--- a/solution.py
+++ b/solution.py
@@ -23,7 +23,9 @@
     grad_scale = 1.0 / math.sqrt(total_tokens)
     grad_all, input_all = (
         lax.all_gather(grad_out, "row", axis=0, tiled=True),
-        lax.all_gather(inputs, "row", axis=0, tiled=True),
+        jnp.concatenate(
+            lax.all_to_all(jnp.stack(lax.axis_size("row") * [inputs], 0), "row", 0, 0), 0
+        ),
     )
     partial_hidden = jnp.einsum(
         "td,fd->tf", grad_all, down_weight, preferred_element_type=jnp.float32

time: 623 us -> 542 us (0.87)
  waiting for transfers between devices: 588 us -> 469 us
  blocking collectives: 0 us -> 37.5 us
    all_gather x1 -> x0, waiting for transfers between devices: 82.4 us -> none  [per_device(): lax.all_gather(inputs, 'row', axis=0, tiled=True)]
    all_to_all x0 -> x1, blocking collectives: none -> 37.5 us  [per_device(): lax.all_to_all(jnp.stack(lax.axis_size('row') * [inputs], 0), 'row', 0, 0)]
    all_gather x1, waiting for transfers between devices: 65.4 us -> 30.3 us  [per_device(): lax.all_gather(hidden, 'col', axis=0, tiled=True)]
  transfers between devices with their start and end apart: 7 -> 6, of which waited for: 7 -> 6; matrix products, arithmetic and copies ran while one was open for 2% -> 2% of each run, Pallas kernels for 0% -> 0%
where the time goes in v1:
time: 542 us
  waiting for transfers between devices  469 us (87%)
  blocking collectives  37.5 us (7%)
  matrix products  14.2 us (3%)
  between operations  14.2 us (3%)
    reduce_scatter x1, waiting for transfers between devices, per_device(): lax.psum_scatter(jnp.einsum('tf,df->td', gate_all, gate_weight, preferred...  128 us
    all_gather x1, waiting for transfers between devices, per_device(): lax.all_gather(grad_out, 'row', axis=0, tiled=True)  90.3 us
    reduce_scatter x1, waiting for transfers between devices, per_device(): lax.psum_scatter(partial_hidden, 'col', scatter_dimension=0, tiled=True)  76.2 us
    all_gather x1, waiting for transfers between devices, per_device(): lax.all_gather(up_term, 'col', axis=0, tiled=True)  72.6 us
    all_gather x1, waiting for transfers between devices, per_device(): lax.all_gather(gate_term, 'col', axis=0, tiled=True)  69.8 us
    all_to_all x1, blocking collectives, per_device(): lax.all_to_all(jnp.stack(lax.axis_size('row') * [inputs], 0), 'row', 0, 0)  37.5 us
    all_gather x1, waiting for transfers between devices, per_device(): lax.all_gather(hidden, 'col', axis=0, tiled=True)  30.3 us
  transfers between devices with their start and end apart: 6, of which 6 were waited for; matrix products, arithmetic and copies ran while one was open for 2% of the time, Pallas kernels for 0%

profile of v1, /device:TPU:16, one launch (start us, length us, event | category | flops | bytes accessed | tf_op | source)
XLA Modules:
  0.0 541.6 jit_solution(14331241377043208874)
XLA Ops:
  7.2 0.7 all-gather.5.cloned.1.call-update
  8.0 90.3 %all-gather.5.cloned.1.call-done = bf16[1024,512]{1,0:T(8,128)(2,1)} async-done(((bf16[32,512]{1,0:T(8,128)(2,1)}), bf16[1024,512]{1,0:T(8,128)(2,1)}) %all-gather.5.cloned.1.call-update) | async-done | bytes 1048592 | tf_op jit(solution)/shard_map/all_gather | solution.py:25
  98.3 3.3 fusion.13
  101.6 0.0 all-gather.7.cloned.1.call-start
  101.7 76.2 %reduce-scatter.3.cloned.1.call-done = f32[64,512]{1,0:T(8,128)} async-done(((f32[1024,512]{1,0:T(8,128)}), f32[64,512]{1,0:T(8,128)}) %reduce-scatter.3.cloned.1.call-update) | async-done | bytes 131088 | tf_op jit(solution)/shard_map/reduce_scatter | solution.py:33
  177.9 1.7 multiply_convert_fusion
  179.6 0.0 all-gather.9.cloned.1.call-start
  179.7 0.5 all-gather.9.cloned.1.call-update
  180.2 0.5 all-gather.11.cloned.1.call-update
  180.8 69.8 %all-gather.7.cloned.1.call-done = bf16[1024,512]{1,0:T(8,128)(2,1)} async-done(((bf16[64,512]{1,0:T(8,128)(2,1)}), bf16[1024,512]{1,0:T(8,128)(2,1)}) %all-gather.7.cloned.1.call-update) | async-done | bytes 1048592 | tf_op jit(solution)/shard_map/all_gather | solution.py:37
  250.6 2.0 fusion.14
  252.6 72.6 %all-gather.9.cloned.1.call-done = bf16[1024,512]{1,0:T(8,128)(2,1)} async-done(((bf16[64,512]{1,0:T(8,128)(2,1)}), bf16[1024,512]{1,0:T(8,128)(2,1)}) %all-gather.9.cloned.1.call-update) | async-done | bytes 1048592 | tf_op jit(solution)/shard_map/all_gather | solution.py:38
  325.2 3.4 convolution_add_fusion
  328.7 0.7 copy-done.6
  329.4 0.1 stack.2
  329.5 37.5 %all_to_all.5 = bf16[32,32,512]{2,1,0:T(8,128)(2,1)S(1)} all-to-all(bf16[32,32,512]{2,1,0:T(8,128)(2,1)S(1)} %stack.2), channel_id=1, replica_groups=mesh['col'=16,'row'=32] {'row'}, dimensions={0} | all-to-all | bytes 2097152 | tf_op jit(solution)/shard_map/all_to_all | solution.py:27
  367.0 0.7 fusion.4
  367.7 1.0 copy.11
  368.7 2.0 fusion.3
  370.8 1.0 copy.12
  371.8 30.3 %all-gather.11.cloned.1.call-done = bf16[1024,512]{1,0:T(8,128)(2,1)} async-done(((bf16[64,512]{1,0:T(8,128)(2,1)}), bf16[1024,512]{1,0:T(8,128)(2,1)}) %all-gather.11.cloned.1.call-update) | async-done | bytes 1048592 | tf_op jit(solution)/shard_map/all_gather | solution.py:36
  402.1 2.8 fusion.2
  404.8 128.4 %reduce-scatter.5.cloned.1.call-done = f32[32,512]{1,0:T(8,128)} async-done(((f32[1024,512]{1,0:T(8,128)}), f32[32,512]{1,0:T(8,128)}) %reduce-scatter.5.cloned.1.call-update) | async-done | bytes 65552 | tf_op jit(solution)/shard_map/reduce_scatter | solution.py:48
  533.3 1.5 convert_element_type.37
  (20 shorter events, 0.2 us)
Async XLA Ops:
  7.2 91.1 %copy-start = (bf16[512,512]{1,0:T(8,128)(2,1)S(1)}, bf16[512,512]{1,0:T(8,128)(2,1)}, u32[]{:S(2)}) copy-start(bf16[512,512]{1,0:T(8,128)(2,1)} %param.13) | copy-start | bytes 1572868
  7.2 91.1 %all-gather.5.cloned.1.call-start = ((), (), s32[]{:S(2)}) async-start(), calls=%async_computation.3 | async-start | bytes 1081344 | tf_op jit(solution)/shard_map/all_gather | solution.py:25
  7.9 170.0 %copy-start.4 = (bf16[64,512]{1,0:T(8,128)(2,1)S(1)}, bf16[64,512]{1,0:T(8,128)(2,1)}, u32[]{:S(2)}) copy-start(bf16[64,512]{1,0:T(8,128)(2,1)} %param.9) | copy-start | bytes 196612
  7.9 170.0 %copy-start.5 = (bf16[64,512]{1,0:T(8,128)(2,1)S(1)}, bf16[64,512]{1,0:T(8,128)(2,1)}, u32[]{:S(2)}) copy-start(bf16[64,512]{1,0:T(8,128)(2,1)} %param.10) | copy-start | bytes 196612
  7.9 170.0 %reduce-scatter.3.cloned.1.call-start = ((), (), s32[]{:S(2)}) async-start(), calls=%async_computation.4 | async-start | bytes 2228224 | tf_op jit(solution)/shard_map/reduce_scatter | solution.py:33
  101.6 149.0 %copy-start.3 = (bf16[512,512]{1,0:T(8,128)(2,1)S(1)}, bf16[512,512]{1,0:T(8,128)(2,1)}, u32[]{:S(2)}) copy-start(bf16[512,512]{1,0:T(8,128)(2,1)} %param.11) | copy-start | bytes 1572868
  101.6 149.0 %all-gather.7.cloned.1.call-start = ((), (), s32[]{:S(2)}) async-start(), calls=%async_computation.5 | async-start | bytes 1114112 | tf_op jit(solution)/shard_map/all_gather | solution.py:37
  179.6 145.6 %all-gather.9.cloned.1.call-start = ((), (), s32[]{:S(2)}) async-start(), calls=%async_computation.6 | async-start | bytes 1114112 | tf_op jit(solution)/shard_map/all_gather | solution.py:38
  180.2 221.9 %all-gather.11.cloned.1.call-start = ((), (), s32[]{:S(2)}) async-start(), calls=%async_computation.8 | async-start | bytes 1114112 | tf_op jit(solution)/shard_map/all_gather | solution.py:36
  180.8 352.5 %reduce-scatter.5.cloned.1.call-start = ((), (), s32[]{:S(2)}) async-start(), calls=%async_computation.7 | async-start | bytes 2162688 | tf_op jit(solution)/shard_map/reduce_scatter | solution.py:48
  328.6 0.8 copy-start.6
  329.4 37.6 %copy-start.2 = (bf16[1024,512]{1,0:T(8,128)(2,1)S(1)}, bf16[1024,512]{1,0:T(8,128)(2,1)}, u32[]{:S(2)}) copy-start(bf16[1024,512]{1,0:T(8,128)(2,1)} %all-gather.7.cloned.1.call-done) | copy-start | bytes 3145732
  368.7 33.3 %copy-start.1 = (bf16[1024,512]{1,0:T(8,128)(2,1)S(1)}, bf16[1024,512]{1,0:T(8,128)(2,1)}, u32[]{:S(2)}) copy-start(bf16[1024,512]{1,0:T(8,128)(2,1)} %all-gather.5.cloned.1.call-done) | copy-start | bytes 3145732
Sparse Core Ops, SparseCore 0:
  11.4 86.8 all-gather.4
  101.8 76.1 reduce-scatter.2
  180.6 69.9 all-gather.6
  253.1 72.0 all-gather.8
  327.1 74.9 all-gather.10
  406.7 126.5 reduce-scatter.4
